TPU v7x, 32 devices: a whole 2x2x4 slice. The times are simulated.
32 devices in a mesh: freq: 4 (over z), tm: 4 (over x, core), grp: 2 (over y).
Axes of the slice: x: 2, y: 2, z: 4, core: 2. Of those that a mesh axis runs over, the one named last changes fastest.
Arguments:
- voltages: bfloat16 [4, 2, 1024, 4096], P(None, None, ('freq', 'grp'), 'tm'), may hold values from -6 to 6
- prior_gains: float32 [4, 2, 1024], P('freq'), may hold values from -4.2 to 4.2
- station_flags: int32 [512], replicated, may hold values 0 or 1
- ingest_map: int32 [512], replicated, may hold values from 0 to 511, each once
- station_coords: float32 [2, 512], replicated, may hold values from -40 to 40
- pointing: int32 [2, 256], replicated, may hold values from 0 to 63
- corr_channels: int32 [4], replicated, may hold values from 0 to 3, each once
- beam_channels: int32 [4], replicated, may hold values from 0 to 3, each once
Outputs:
- visibilities: float32 [4, 2, 1024, 1024], P('freq', None, 'grp', 'tm')
- solved_gains: float32 [4, 2, 1024], P('freq')
- tied_beams: bfloat16 [4, 2, 2, 256, 4096], P('freq', None, None, 'grp', 'tm')
Inputs may be any that keep to these rules, and one draw needn't show every extreme that they name: `ingest_map`: each station appears in exactly one ingest slot. `corr_channels`: each channel is handled by exactly one correlator slot. `beam_channels`: each channel is handled by exactly one beamformer slot.
All inputs are finite; a program needn't handle non-finite values.
Results may differ from a plain program's by a relative error of at most 0.0049.
Values may be sent and summed in bfloat16 or wider, within the bound.
A program may use at most 64 MiB of HBM per device.

v0:
```python
import math
import jax
import jax.numpy as jnp
from jax import lax
from jax.sharding import PartitionSpec as P

S = 512
ITERS = 4
grid_cells = 64.0


def weights_for(gains_sel, ratio, pointing_part, slot_coords):
    east_dir = (pointing_part[0].astype(jnp.float32) + 0.5) / grid_cells - 0.5
    north_dir = (pointing_part[1].astype(jnp.float32) + 0.5) / grid_cells - 0.5
    phase = (
        2.0
        * math.pi
        * ratio
        * (
            east_dir[:, None] * slot_coords[0][None, :]
            + north_dir[:, None] * slot_coords[1][None, :]
        )
    )
    cosine = jnp.cos(phase)
    sine = jnp.sin(phase)
    gain_real = gains_sel[0].reshape(2, S)
    gain_imag = gains_sel[1].reshape(2, S)
    denom = jnp.maximum(gain_real * gain_real + gain_imag * gain_imag, 0.5)
    along_real = gain_real / denom
    along_imag = gain_imag / denom
    factor = 1.0 / math.sqrt(S)
    w_real = (cosine[None] * along_real[:, None, :] - sine[None] * along_imag[:, None, :]) * factor
    w_imag = -(cosine[None] * along_imag[:, None, :] + sine[None] * along_real[:, None, :]) * factor
    upper = jnp.stack([w_real, -w_imag], axis=2)
    lower = jnp.stack([w_imag, w_real], axis=2)
    return jnp.stack([upper, lower], axis=1).astype(jnp.bfloat16)


def body(
    voltages,
    prior_gains,
    station_flags,
    ingest_map,
    station_coords,
    pointing,
    corr_channels,
    beam_channels,
):
    highest = lax.Precision.HIGHEST
    n_freq = lax.axis_size("freq")
    n_time = lax.axis_size("tm")
    n_group = lax.axis_size("grp")
    freq_index = lax.axis_index("freq")
    time_index = lax.axis_index("tm")
    group_index = lax.axis_index("grp")
    channels_all = voltages.shape[0]
    per_device = channels_all // n_freq
    per_input = voltages.shape[2]
    samples = voltages.shape[3]
    inputs_all = 2 * S
    corr_source = jnp.take(voltages, corr_channels, axis=0)
    beam_source = jnp.take(voltages, beam_channels, axis=0)
    corr_half, beam_half = (
        lax.all_to_all(corr_source, "freq", split_axis=0, concat_axis=2, tiled=True),
        lax.all_to_all(beam_source, "freq", split_axis=0, concat_axis=2, tiled=True),
    )
    split_shape = (per_device, 2, n_freq, per_input, samples)
    corr_pair, beam_pair = (
        lax.all_gather(corr_half.reshape(split_shape), "grp", axis=3, tiled=True),
        lax.all_gather(beam_half.reshape(split_shape), "grp", axis=3, tiled=True),
    )
    full_shape = (per_device, 2, inputs_all, samples)
    corr_volts = corr_pair.reshape(full_shape)
    beam_volts = beam_pair.reshape(full_shape)
    slot_keep = 1 - jnp.take(station_flags, ingest_map)
    keep = jnp.concatenate([slot_keep, slot_keep]).astype(jnp.bfloat16)
    corr_volts = corr_volts * keep[None, None, :, None]
    beam_volts = beam_volts * keep[None, None, :, None]
    rows = inputs_all // n_group
    row_start = group_index * rows
    mine = lax.dynamic_slice_in_dim(corr_volts, row_start, rows, 2)
    left = jnp.stack([mine, jnp.stack([mine[:, 1], -mine[:, 0]], axis=1)], axis=1)
    partial_value = jnp.einsum(
        "corit,crjt->coij", left, corr_volts, preferred_element_type=jnp.float32
    )
    partial_value = partial_value * (1.0 / (samples * n_time))
    columns = inputs_all // n_time
    vis_block = lax.psum_scatter(partial_value, "tm", scatter_dimension=3, tiled=True)
    gains = prior_gains
    for iteration in range(ITERS):
        power = jnp.sum(gains * gains, axis=(1, 2)) + 1e-06
        along = lax.dynamic_slice_in_dim(gains, time_index * columns, columns, 2)
        real_real = jnp.einsum("cij,cj->ci", vis_block[:, 0], along[:, 0], precision=highest)
        imag_imag = jnp.einsum("cij,cj->ci", vis_block[:, 1], along[:, 1], precision=highest)
        real_imag = jnp.einsum("cij,cj->ci", vis_block[:, 0], along[:, 1], precision=highest)
        imag_real = jnp.einsum("cij,cj->ci", vis_block[:, 1], along[:, 0], precision=highest)
        update = jnp.stack([real_real - imag_imag, imag_real + real_imag], axis=1)
        update = lax.psum(update, "tm")
        own_rows = lax.dynamic_slice_in_dim(gains, row_start, rows, 2)
        fresh = 0.5 * (own_rows + inputs_all * update / power[:, None, None])
        gains = lax.all_gather(fresh, "grp", axis=2, tiled=True)
    all_gains = lax.all_gather(gains, "freq", axis=0, tiled=True)
    my_beam = lax.dynamic_slice_in_dim(beam_channels, freq_index * per_device, per_device, 0)
    onehot = (corr_channels[None, :] == my_beam[:, None]).astype(jnp.float32)
    selected = jnp.einsum("ck,kri->cri", onehot, all_gains, precision=highest)
    ratio = 0.875 + 0.25 * (my_beam.astype(jnp.float32) + 0.5) / channels_all
    beams_mine = pointing.shape[1] // n_group
    pointing_part = lax.dynamic_slice_in_dim(pointing, group_index * beams_mine, beams_mine, 1)
    slot_coords = jnp.take(station_coords, ingest_map, axis=1)
    weights = jax.vmap(weights_for, in_axes=(0, 0, None, None))(
        selected, ratio, pointing_part, slot_coords
    )
    block = beam_volts.reshape(per_device, 2, 2, S, samples)
    beams = jnp.einsum("cpobrq,crpqt->cpobt", weights, block, preferred_element_type=jnp.float32)
    return (vis_block, gains, beams.astype(jnp.bfloat16))


def solution(mesh):
    return jax.shard_map(
        body,
        mesh=mesh,
        in_specs=(
            P(None, None, ("freq", "grp"), "tm"),
            P("freq", None, None),
            P(),
            P(),
            P(),
            P(),
            P(),
            P(),
        ),
        out_specs=(
            P("freq", None, "grp", "tm"),
            P("freq", None, None),
            P("freq", None, None, "grp", "tm"),
        ),
        check_vma=False,
    )
```

profile of v0, /device:TPU:0, one launch (start us, length us, event | category | flops | bytes accessed | tf_op | source)
XLA Modules:
  0.0 313.8 jit_solution(3851320219780948037)
XLA Ops:
  7.2 0.8 compare_select_fusion.1
  8.0 0.7 compare_and_fusion
  8.8 2.0 gather_fusion.2
  10.8 1.9 broadcast_select_fusion.1
  12.7 54.4 %all_to_all.30 = bf16[4,2,128,1024]{3,2,1,0:T(8,128)(2,1)} all-to-all(bf16[4,2,128,1024]{3,2,1,0:T(8,128)(2,1)S(1)} %broadcast_select_fusion.1), channel_id=1, replica_groups=mesh['freq'=4,'tm'=4,'grp'=2] {'freq'}, dimensions={0} | all-to-all | bytes 4194304 | tf_op jit(solution)/shard_map/all_to_all | solution.py:64
  67.2 2.0 gather_fusion.3
  69.2 1.9 broadcast_select_fusion
  71.1 50.7 %all_to_all.31 = bf16[4,2,128,1024]{3,2,1,0:T(8,128)(2,1)} all-to-all(bf16[4,2,128,1024]{3,2,1,0:T(8,128)(2,1)S(1)} %broadcast_select_fusion), channel_id=1, replica_groups=mesh['freq'=4,'tm'=4,'grp'=2] {'freq'}, dimensions={0} | all-to-all | bytes 4194304 | tf_op jit(solution)/shard_map/all_to_all | solution.py:65
  121.8 0.6 copy-done.5
  122.5 3.5 %gather_fusion = s32[512]{0:T(512)S(1)} fusion(s32[512]{0:T(512)S(1)} %copy-done.1, s32[1024]{0:T(1024)S(1)} %pad_clamp_fusion.1), kind=kCustom, calls=%fused_computation.2 | custom fusion | bytes 6144 | tf_op jit(solution)/shard_map/jit(_take)/gather | solution.py:75
  126.1 2.5 broadcast_multiply_fusion
  129.1 1.8 copy-done.3
  132.6 6.1 %fusion.5 = f32[1,2,512,1024]{3,2,1,0:T(8,128)} fusion(bf16[2,1024,1024,1]{2,1,0,3:T(8,128)(2,1)S(1)} %bitcast.171, bf16[1,1,2,512,1024]{4,3,2,1,0:T(8,128)(2,1)S(1)} %maximum_bitcast_fusion.4, bf16[1,1,2,512,1024]{4,3,2,1,0:T(8,128)(2,1)S(1)} %fusion.76), kind=kOutput, calls=%fused_computation.11 | convolution fusion | flops 4298113024 | bytes 12582912 | tf_op jit(solution)/shard_map/corit,crjt->coij/dot_general | solution.py:83
  138.8 0.6 copy-done.8
  139.4 0.6 dynamic_slice.42
  140.1 1.0 gather_fusion.1
  141.8 0.6 multiply_reduce_fusion.3
  143.5 1.8 fusion.32
  145.3 36.2 %all-gather.5.cloned.1.call-done = bf16[1,2,4,256,1024]{4,3,1,2,0:T(8,128)(2,1)} async-done(((bf16[1,2,4,128,1024]{4,3,1,2,0:T(8,128)(2,1)}), bf16[1,2,4,256,1024]{4,3,1,2,0:T(8,128)(2,1)}) %all-gather.5.cloned.1.call-update) | async-done | bytes 4194320 | tf_op jit(solution)/shard_map/all_gather | solution.py:70
  181.6 4.6 %copy.27 = bf16[1,2,4,256,1024]{4,3,2,1,0:T(8,128)(2,1)} copy(bf16[1,2,4,256,1024]{4,3,1,2,0:T(8,128)(2,1)} %all-gather.5.cloned.1.call-done) | data formatting | bytes 8388608 | tf_op jit(solution)/shard_map/all_gather | solution.py:70
  186.2 42.9 %reduce-scatter.2.cloned.1.call-done = f32[1,2,512,256]{3,2,1,0:T(8,128)} async-done(((f32[1,2,512,1024]{3,2,1,0:T(8,128)}), f32[1,2,512,256]{3,2,1,0:T(8,128)}) %reduce-scatter.2.cloned.1.call-update) | async-done | bytes 1048592 | tf_op jit(solution)/shard_map/reduce_scatter | solution.py:88
  229.1 1.7 fusion.29
  230.8 1.6 fusion.21
  232.4 1.6 fusion.22
  234.0 1.6 fusion.30
  235.6 5.8 %psum.28 = f32[1,2,512]{2,1,0:T(2,128)S(1)} all-reduce(f32[1,2,512]{2,1,0:T(2,128)S(1)} %pad_maximum_fusion), channel_id=1, replica_groups=mesh['freq'=4,'tm'=4,'grp'=2] {'tm'}, use_global_device_ids=true, to_apply=%region_1.3 | all-reduce | flops 1024 | bytes 8192 | tf_op jit(solution)/shard_map/psum | solution.py:98
  241.4 4.4 %all_gather.22 = f32[1,2,1024]{2,1,0:T(2,128)S(1)} all-gather(f32[1,2,512]{2,1,0:T(2,128)S(1)} %fusion.38), channel_id=1, replica_groups=mesh['freq'=4,'tm'=4,'grp'=2] {'grp'}, dimensions={2}, use_global_device_ids=true | all-gather | bytes 12288 | tf_op jit(solution)/shard_map/all_gather | solution.py:101
  245.8 0.6 multiply_reduce_fusion.2
  246.9 0.6 fusion.19
  247.5 0.6 fusion.20
  248.0 0.6 fusion.28
  248.6 5.7 %psum.29 = f32[1,2,512]{2,1,0:T(2,128)S(1)} all-reduce(f32[1,2,512]{2,1,0:T(2,128)S(1)} %pad_maximum_fusion.1), channel_id=1, replica_groups=mesh['freq'=4,'tm'=4,'grp'=2] {'tm'}, use_global_device_ids=true, to_apply=%region_3.5 | all-reduce | flops 1024 | bytes 8192 | tf_op jit(solution)/shard_map/psum | solution.py:98
  255.0 4.5 %all_gather.23 = f32[1,2,1024]{2,1,0:T(2,128)S(1)} all-gather(f32[1,2,512]{2,1,0:T(2,128)S(1)} %fusion.39), channel_id=1, replica_groups=mesh['freq'=4,'tm'=4,'grp'=2] {'grp'}, dimensions={2}, use_global_device_ids=true | all-gather | bytes 12288 | tf_op jit(solution)/shard_map/all_gather | solution.py:101
  259.5 0.6 multiply_reduce_fusion.1
  260.6 0.6 fusion.17
  261.8 0.6 fusion.26
  262.4 5.7 %psum.30 = f32[1,2,512]{2,1,0:T(2,128)S(1)} all-reduce(f32[1,2,512]{2,1,0:T(2,128)S(1)} %pad_maximum_fusion.2), channel_id=1, replica_groups=mesh['freq'=4,'tm'=4,'grp'=2] {'tm'}, use_global_device_ids=true, to_apply=%region_5.7 | all-reduce | flops 1024 | bytes 8192 | tf_op jit(solution)/shard_map/psum | solution.py:98
  268.7 4.4 %all_gather.24 = f32[1,2,1024]{2,1,0:T(2,128)S(1)} all-gather(f32[1,2,512]{2,1,0:T(2,128)S(1)} %fusion.40), channel_id=1, replica_groups=mesh['freq'=4,'tm'=4,'grp'=2] {'grp'}, dimensions={2}, use_global_device_ids=true | all-gather | bytes 12288 | tf_op jit(solution)/shard_map/all_gather | solution.py:101
  273.1 0.6 multiply_reduce_fusion
  274.2 0.6 fusion.15
  275.3 0.6 fusion.24
  275.9 5.7 %psum.31 = f32[1,2,512]{2,1,0:T(2,128)S(1)} all-reduce(f32[1,2,512]{2,1,0:T(2,128)S(1)} %pad_maximum_fusion.3), channel_id=1, replica_groups=mesh['freq'=4,'tm'=4,'grp'=2] {'tm'}, use_global_device_ids=true, to_apply=%region_7.9 | all-reduce | flops 1024 | bytes 8192 | tf_op jit(solution)/shard_map/psum | solution.py:98
  282.3 4.4 %all_gather.25 = f32[1,2,1024]{2,1,0:T(2,128)S(1)} all-gather(f32[1,2,512]{2,1,0:T(2,128)S(1)} %fusion.41), channel_id=1, replica_groups=mesh['freq'=4,'tm'=4,'grp'=2] {'grp'}, dimensions={2}, use_global_device_ids=true | all-gather | bytes 12288 | tf_op jit(solution)/shard_map/all_gather | solution.py:101
  286.6 13.4 %all_gather.26 = f32[4,2,1024]{2,1,0:T(2,128)S(1)} all-gather(f32[1,2,1024]{2,1,0:T(2,128)S(1)} %all_gather.25), channel_id=1, replica_groups=mesh['freq'=4,'tm'=4,'grp'=2] {'freq'}, dimensions={0}, use_global_device_ids=true | all-gather | bytes 40960 | tf_op jit(solution)/shard_map/all_gather | solution.py:102
  300.0 0.8 fusion.33
  300.9 1.1 negate_convert_fusion
  302.1 4.6 %fusion.8 = bf16[1,2,2,128,1024]{4,3,2,1,0:T(8,128)(2,1)} fusion(bf16[2,1,128,2,512]{4,2,3,1,0:T(8,128)(2,1)S(1)} %get-tuple-element.17, bf16[2,1,128,2,512]{4,2,3,1,0:T(8,128)(2,1)S(1)} %get-tuple-element.16, bf16[2,2,512,1024]{3,2,1,0:T(8,128)(2,1)} %bitcast.170, bf16[2,512]{1,0:T(2,128)(2,1)S(1)} %convert_element_type.50), kind=kOutput, calls=%fused_computation.19 | convolution fusion | flops 1076887552 | bytes 6293504 | tf_op jit(solution)/shard_map/cpobrq,crpqt->cpobt/dot_general | solution.py:114
  306.6 0.6 copy.47
  (71 shorter events, 6.1 us)
Async XLA Ops:
  7.2 1.6 copy-start
  7.2 118.9 %all-gather.3.cloned.1.call-start = ((), (), s32[]{:S(2)}) async-start(), calls=%async_computation.3 | async-start | bytes 6291456 | tf_op jit(solution)/shard_map/all_gather | solution.py:69
  67.2 114.4 %all-gather.5.cloned.1.call-start = ((), (), s32[]{:S(2)}) async-start(), calls=%async_computation.5 | async-start | bytes 6291456 | tf_op jit(solution)/shard_map/all_gather | solution.py:70
  121.8 0.7 copy-start.5
  121.8 0.7 copy-start.1
  121.8 107.3 %reduce-scatter.2.cloned.1.call-start = ((), (), s32[]{:S(2)}) async-start(), calls=%async_computation.4 | async-start | bytes 5242880 | tf_op jit(solution)/shard_map/reduce_scatter | solution.py:88
  128.7 2.3 copy-start.3
  138.7 0.7 copy-start.8
  138.7 1.3 copy-start.7
  138.7 3.1 copy-start.4
  138.7 4.3 %copy-start.9 = (s32[2,256]{1,0:T(2,128)S(1)}, s32[2,256]{1,0:T(2,128)}, u32[]{:S(2)}) copy-start(s32[2,256]{1,0:T(2,128)} %param.15) | copy-start | bytes 6148
  229.1 17.3 %copy-start.2 = (f32[1,2,512,256]{3,2,1,0:T(8,128)S(1)}, f32[1,2,512,256]{3,2,1,0:T(8,128)}, u32[]{:S(2)}) copy-start(f32[1,2,512,256]{3,2,1,0:T(8,128)} %reduce-scatter.2.cloned.1.call-done) | copy-start | bytes 3145732
  260.1 39.9 %copy-start.6 = (s32[4]{0:T(128)S(1)}, s32[4]{0:T(128)}, u32[]{:S(2)}) copy-start(s32[4]{0:T(128)} %param.16) | copy-start | bytes 52
Sparse Core Ops, SparseCore 0:
  67.3 55.9 all-gather.2
  124.8 56.7 all-gather.4
  184.7 44.3 reduce-scatter.1
where the time goes:
time: 315 us; the launch traced here: 314 us
  blocking collectives  159 us (50%)
  waiting for transfers between devices  79.2 us (25%)
  matrix products  24.5 us (8%)
  local copies, waits for them, and re-layouts  19 us (6%)
  between operations  17.3 us (5%)
  other arithmetic  14.7 us (5%)
    all_to_all x1, blocking collectives, body(): lax.all_to_all(corr_source, 'freq', split_axis=0, concat_axis=2, tiled=True)  54.4 us
    all_to_all x1, blocking collectives, body(): lax.all_to_all(beam_source, 'freq', split_axis=0, concat_axis=2, tiled=True)  50.7 us
    reduce_scatter x1, waiting for transfers between devices, body(): lax.psum_scatter(partial_value, 'tm', scatter_dimension=3, tiled=True)  42.9 us
    all_gather x1, waiting for transfers between devices, body(): lax.all_gather(beam_half.reshape(split_shape), 'grp', axis=3, tiled=True)  36.2 us
    psum x4, blocking collectives, body(): update = lax.psum(update, 'tm')  22.8 us
    all_gather x4, blocking collectives, body(): gains = lax.all_gather(fresh, 'grp', axis=2, tiled=True)  17.6 us
    all_gather x1, blocking collectives, body(): all_gains = lax.all_gather(gains, 'freq', axis=0, tiled=True)  13.4 us
  transfers between devices with their start and end apart: 3, of which 2 were waited for; matrix products, arithmetic and copies ran while one was open for 9% of the time, Pallas kernels for 0%

commit v1 on v0

--- a/solution.py
+++ b/solution.py
@@ -7,6 +7,15 @@
 S = 512
 ITERS = 4
 grid_cells = 64.0
+
+
+def doubling_sum(x, axis):
+    n_dev = lax.axis_size(axis)
+    summed, stride = (x, 1)
+    while stride < n_dev:
+        summed = summed + lax.ppermute(summed, axis, [(i, i ^ stride) for i in range(n_dev)])
+        stride = 2 * stride
+    return summed
 
 
 def weights_for(gains_sel, ratio, pointing_part, slot_coords):
@@ -95,7 +104,7 @@
         real_imag = jnp.einsum("cij,cj->ci", vis_block[:, 0], along[:, 1], precision=highest)
         imag_real = jnp.einsum("cij,cj->ci", vis_block[:, 1], along[:, 0], precision=highest)
         update = jnp.stack([real_real - imag_imag, imag_real + real_imag], axis=1)
-        update = lax.psum(update, "tm")
+        update = doubling_sum(update, "tm")
         own_rows = lax.dynamic_slice_in_dim(gains, row_start, rows, 2)
         fresh = 0.5 * (own_rows + inputs_all * update / power[:, None, None])
         gains = lax.all_gather(fresh, "grp", axis=2, tiled=True)

time: 315 us -> 289 us (0.917)
  blocking collectives: 159 us -> 85.6 us
  waiting for transfers between devices: 79.2 us -> 118 us
  starting transfers between devices: 0.12 us -> 10.1 us
    all_gather x1, waiting for transfers between devices: 0.01 us -> 51.8 us  [body(): lax.all_gather(corr_half.reshape(split_shape), 'grp', axis=3, tiled=True)]
    all_to_all x1 -> x0, blocking collectives: 50.7 us -> none  [body(): lax.all_to_all(beam_source, 'freq', split_axis=0, concat_axis=2, tiled=True)]
    psum x4 -> x0, blocking collectives: 22.8 us -> none  [body(): update = lax.psum(update, 'tm')]
    all_gather x1, waiting for transfers between devices: 36.2 us -> 23.4 us  [body(): lax.all_gather(beam_half.reshape(split_shape), 'grp', axis=3, tiled=True)]
    reduce_scatter x1, waiting for transfers between devices: 42.9 us -> 33.2 us  [body(): lax.psum_scatter(partial_value, 'tm', scatter_dimension=3, tiled=True)]
    ppermute x0 -> x8, starting transfers between devices: none -> 5.3 us  [doubling_sum(): lax.ppermute(summed, axis, [(i, i ^ stride) for i in range(n_dev)])]
    all_to_all x0 -> x1, waiting for transfers between devices: none -> 4.82 us  [body(): lax.all_to_all(beam_source, 'freq', split_axis=0, concat_axis=2, tiled=True)]
    all_to_all x0 -> x1, starting transfers between devices: none -> 4.76 us  [body(): lax.all_to_all(beam_source, 'freq', split_axis=0, concat_axis=2, tiled=True)]
  transfers between devices with their start and end apart: 3 -> 12, of which waited for: 2 -> 9; matrix products, arithmetic and copies ran while one was open for 9% -> 11% of each run, Pallas kernels for 0% -> 0%
where the time goes in v1:
time: 289 us; the launch traced here: 288 us
  waiting for transfers between devices  118 us (41%)
  blocking collectives  85.6 us (30%)
  matrix products  24.5 us (8%)
  local copies, waits for them, and re-layouts  20.5 us (7%)
  between operations  17.4 us (6%)
  other arithmetic  12.2 us (4%)
  starting transfers between devices  10.1 us (3%)
    all_to_all x1, blocking collectives, body(): lax.all_to_all(corr_source, 'freq', split_axis=0, concat_axis=2, tiled=True)  54.4 us
    all_gather x1, waiting for transfers between devices, body(): lax.all_gather(corr_half.reshape(split_shape), 'grp', axis=3, tiled=True)  51.8 us
    reduce_scatter x1, waiting for transfers between devices, body(): lax.psum_scatter(partial_value, 'tm', scatter_dimension=3, tiled=True)  33.2 us
    all_gather x1, waiting for transfers between devices, body(): lax.all_gather(beam_half.reshape(split_shape), 'grp', axis=3, tiled=True)  23.4 us
    all_gather x4, blocking collectives, body(): gains = lax.all_gather(fresh, 'grp', axis=2, tiled=True)  18 us
    all_gather x1, blocking collectives, body(): all_gains = lax.all_gather(gains, 'freq', axis=0, tiled=True)  13.2 us
    dot_general x1, matrix products, body(): jnp.einsum('corit,crjt->coij', left, corr_volts, preferred_element_type=j...  6.09 us
  transfers between devices with their start and end apart: 12, of which 9 were waited for; matrix products, arithmetic and copies ran while one was open for 11% of the time, Pallas kernels for 0%

profile of v1, /device:TPU:0, one launch (start us, length us, event | category | flops | bytes accessed | tf_op | source)
XLA Modules:
  0.0 287.9 jit_solution(13810967356538818061)
XLA Ops:
  7.2 0.8 compare_select_fusion.1
  8.0 0.7 compare_and_fusion
  8.8 2.0 gather_fusion.2
  10.8 1.9 broadcast_select_fusion.1
  12.7 54.4 %all_to_all.30 = bf16[4,2,128,1024]{3,2,1,0:T(8,128)(2,1)} all-to-all(bf16[4,2,128,1024]{3,2,1,0:T(8,128)(2,1)S(1)} %broadcast_select_fusion.1), channel_id=1, replica_groups=mesh['freq'=4,'tm'=4,'grp'=2] {'freq'}, dimensions={0} | all-to-all | bytes 4194304 | tf_op jit(solution)/shard_map/all_to_all | solution.py:73
  67.2 0.6 copy-done.5
  67.8 3.5 %gather_fusion = s32[512]{0:T(512)S(1)} fusion(s32[512]{0:T(512)S(1)} %copy-done.1, s32[1024]{0:T(1024)S(1)} %pad_clamp_fusion.1), kind=kCustom, calls=%fused_computation.2 | custom fusion | bytes 6144 | tf_op jit(solution)/shard_map/jit(_take)/gather | solution.py:84
  71.5 51.8 %all-gather.3.cloned.1.call-done = bf16[1,2,4,256,1024]{4,3,1,2,0:T(8,128)(2,1)} async-done(((bf16[1,2,4,128,1024]{4,3,1,2,0:T(8,128)(2,1)}), bf16[1,2,4,256,1024]{4,3,1,2,0:T(8,128)(2,1)}) %all-gather.3.cloned.1.call-update) | async-done | bytes 4194320 | tf_op jit(solution)/shard_map/all_gather | solution.py:78
  123.3 2.6 copy.23
  126.7 1.8 copy-done.3
  129.6 6.1 %fusion.5 = f32[1,2,512,1024]{3,2,1,0:T(8,128)} fusion(bf16[2,1024,1024,1]{2,1,0,3:T(8,128)(2,1)S(1)} %bitcast.170, bf16[1,1,2,512,1024]{4,3,2,1,0:T(8,128)(2,1)S(1)} %maximum_bitcast_fusion.4, bf16[1,1,2,512,1024]{4,3,2,1,0:T(8,128)(2,1)S(1)} %fusion.80), kind=kOutput, calls=%fused_computation.11 | convolution fusion | flops 4298113024 | bytes 12582912 | tf_op jit(solution)/shard_map/corit,crjt->coij/dot_general | solution.py:92
  135.8 2.0 gather_fusion.3
  137.8 3.2 %broadcast_select_fusion = bf16[4,2,128,1024]{3,2,1,0:T(8,128)(2,1)} fusion(bf16[4,2,128,1024]{3,2,1,0:T(8,128)(2,1)} %gather_fusion.3, pred[4]{0:T(512)(128)(4,1)S(1)} %get-tuple-element.26), kind=kLoop, calls=%fused_computation.17 | loop fusion | flops 1048576 | bytes 4194308 | tf_op jit(solution)/shard_map/jit(_take)/select_n | solution.py:71
  141.0 4.8 %all-to-all-start.1 = ((bf16[4,2,128,1024]{3,2,1,0:T(8,128)(2,1)}), bf16[4,2,128,1024]{3,2,1,0:T(8,128)(2,1)}, u32[]{:S(2)}, u32[]{:S(2)}) async-start(bf16[4,2,128,1024]{3,2,1,0:T(8,128)(2,1)} %broadcast_select_fusion), calls=%async_computation.2 | async-start | bytes 4194304 | tf_op jit(solution)/shard_map/all_to_all | solution.py:74
  145.9 1.0 gather_fusion.1
  147.1 33.2 %reduce-scatter.2.cloned.1.call-done = f32[1,2,512,256]{3,2,1,0:T(8,128)} async-done(((f32[1,2,512,1024]{3,2,1,0:T(8,128)}), f32[1,2,512,256]{3,2,1,0:T(8,128)}) %reduce-scatter.2.cloned.1.call-update) | async-done | bytes 1048592 | tf_op jit(solution)/shard_map/reduce_scatter | solution.py:97
  180.3 1.7 fusion.29
  182.0 1.6 fusion.21
  183.6 1.6 fusion.22
  185.2 1.6 fusion.30
  186.9 0.6 multiply_reduce_fusion.3
  189.1 4.8 %all-to-all-done.1 = bf16[4,2,128,1024]{3,2,1,0:T(8,128)(2,1)} async-done(((bf16[4,2,128,1024]{3,2,1,0:T(8,128)(2,1)}), bf16[4,2,128,1024]{3,2,1,0:T(8,128)(2,1)}, u32[]{:S(2)}, u32[]{:S(2)}) %all-to-all-start.1) | async-done | bytes 2097184 | tf_op jit(solution)/shard_map/all_to_all | solution.py:74
  194.0 4.4 %all_gather.22 = f32[1,2,1024]{2,1,0:T(2,128)S(1)} all-gather(f32[1,2,512]{2,1,0:T(2,128)S(1)} %fusion.38), channel_id=1, replica_groups=mesh['freq'=4,'tm'=4,'grp'=2] {'grp'}, dimensions={2}, use_global_device_ids=true | all-gather | bytes 12288 | tf_op jit(solution)/shard_map/all_gather | solution.py:110
  198.9 0.6 fusion.19
  200.0 0.6 fusion.28
  200.7 1.1 collective-permute-done.2
  201.9 1.5 collective-permute-start.3
  203.4 0.6 multiply_reduce_fusion.2
  204.7 0.9 collective-permute-done.3
  205.6 4.8 %all_gather.23 = f32[1,2,1024]{2,1,0:T(2,128)S(1)} all-gather(f32[1,2,512]{2,1,0:T(2,128)S(1)} %fusion.39), channel_id=1, replica_groups=mesh['freq'=4,'tm'=4,'grp'=2] {'grp'}, dimensions={2}, use_global_device_ids=true | all-gather | bytes 12288 | tf_op jit(solution)/shard_map/all_gather | solution.py:110
  210.9 0.6 fusion.17
  212.0 0.6 fusion.26
  213.0 0.6 dynamic_slice.42
  214.2 1.5 collective-permute-start.5
  215.8 0.6 multiply_reduce_fusion.1
  217.0 0.9 collective-permute-done.5
  217.9 4.6 %all_gather.24 = f32[1,2,1024]{2,1,0:T(2,128)S(1)} all-gather(f32[1,2,512]{2,1,0:T(2,128)S(1)} %fusion.40), channel_id=1, replica_groups=mesh['freq'=4,'tm'=4,'grp'=2] {'grp'}, dimensions={2}, use_global_device_ids=true | all-gather | bytes 12288 | tf_op jit(solution)/shard_map/all_gather | solution.py:110
  224.8 1.0 fusion.32
  225.9 23.4 %all-gather.5.cloned.1.call-done = bf16[1,2,4,256,1024]{4,3,1,2,0:T(8,128)(2,1)} async-done(((bf16[1,2,4,128,1024]{4,3,1,2,0:T(8,128)(2,1)}), bf16[1,2,4,256,1024]{4,3,1,2,0:T(8,128)(2,1)}) %all-gather.5.cloned.1.call-update) | async-done | bytes 4194320 | tf_op jit(solution)/shard_map/all_gather | solution.py:79
  249.2 4.6 %copy.27 = bf16[1,2,4,256,1024]{4,3,2,1,0:T(8,128)(2,1)} copy(bf16[1,2,4,256,1024]{4,3,1,2,0:T(8,128)(2,1)} %all-gather.5.cloned.1.call-done) | data formatting | bytes 8388608 | tf_op jit(solution)/shard_map/all_gather | solution.py:79
  253.9 1.6 collective-permute-start.7
  255.4 0.6 multiply_reduce_fusion
  256.7 0.9 collective-permute-done.7
  257.6 4.4 %all_gather.25 = f32[1,2,1024]{2,1,0:T(2,128)S(1)} all-gather(f32[1,2,512]{2,1,0:T(2,128)S(1)} %fusion.41), channel_id=1, replica_groups=mesh['freq'=4,'tm'=4,'grp'=2] {'grp'}, dimensions={2}, use_global_device_ids=true | all-gather | bytes 12288 | tf_op jit(solution)/shard_map/all_gather | solution.py:110
  261.9 13.2 %all_gather.26 = f32[4,2,1024]{2,1,0:T(2,128)S(1)} all-gather(f32[1,2,1024]{2,1,0:T(2,128)S(1)} %all_gather.25), channel_id=1, replica_groups=mesh['freq'=4,'tm'=4,'grp'=2] {'freq'}, dimensions={0}, use_global_device_ids=true | all-gather | bytes 40960 | tf_op jit(solution)/shard_map/all_gather | solution.py:111
  275.1 0.8 fusion.33
  276.2 4.6 %fusion.8 = bf16[1,2,2,128,1024]{4,3,2,1,0:T(8,128)(2,1)} fusion(bf16[2,1,128,2,512]{4,2,3,1,0:T(8,128)(2,1)S(1)} %get-tuple-element.17, bf16[2,1,128,2,512]{4,2,3,1,0:T(8,128)(2,1)S(1)} %get-tuple-element.16, bf16[2,2,512,1024]{3,2,1,0:T(8,128)(2,1)} %bitcast.169, bf16[2,512]{1,0:T(2,128)(2,1)S(1)} %convert_element_type.50), kind=kOutput, calls=%fused_computation.19 | convolution fusion | flops 1076887552 | bytes 6293504 | tf_op jit(solution)/shard_map/cpobrq,crpqt->cpobt/dot_general | solution.py:123
  280.8 0.6 copy.47
  (88 shorter events, 9.1 us)
Async XLA Ops:
  7.2 1.6 copy-start
  7.2 116.1 %all-gather.3.cloned.1.call-start = ((), (), s32[]{:S(2)}) async-start(), calls=%async_computation.3 | async-start | bytes 6291456 | tf_op jit(solution)/shard_map/all_gather | solution.py:78
  67.1 0.7 copy-start.5
  67.1 0.7 copy-start.1
  67.1 113.2 %reduce-scatter.2.cloned.1.call-start = ((), (), s32[]{:S(2)}) async-start(), calls=%async_computation.4 | async-start | bytes 5242880 | tf_op jit(solution)/shard_map/reduce_scatter | solution.py:97
  126.3 2.2 copy-start.3
  141.0 4.8 %copy-start.7 = (f32[2,512]{1,0:T(2,128)S(1)}, f32[2,512]{1,0:T(2,128)}, u32[]{:S(2)}) copy-start(f32[2,512]{1,0:T(2,128)} %param.14) | copy-start | bytes 12292
  141.0 39.4 %copy-start.4 = (f32[1,2,1024]{2,1,0:T(2,128)S(1)}, f32[1,2,1024]{2,1,0:T(2,128)}, u32[]{:S(2)}) copy-start(f32[1,2,1024]{2,1,0:T(2,128)} %param.11) | copy-start | bytes 24580
  141.0 53.0 %all-to-all-start.1 = ((bf16[4,2,128,1024]{3,2,1,0:T(8,128)(2,1)}), bf16[4,2,128,1024]{3,2,1,0:T(8,128)(2,1)}, u32[]{:S(2)}, u32[]{:S(2)}) async-start(bf16[4,2,128,1024]{3,2,1,0:T(8,128)(2,1)} %broadcast_select_fusion), calls=%async_computation.2 | async-start | bytes 4194304 | tf_op jit(solution)/shard_map/all_to_all | solution.py:74
  145.8 42.7 %copy-start.9 = (s32[2,256]{1,0:T(2,128)S(1)}, s32[2,256]{1,0:T(2,128)}, u32[]{:S(2)}) copy-start(s32[2,256]{1,0:T(2,128)} %param.15) | copy-start | bytes 6148
  145.8 103.5 %all-gather.5.cloned.1.call-start = ((), (), s32[]{:S(2)}) async-start(), calls=%async_computation.5 | async-start | bytes 6291456 | tf_op jit(solution)/shard_map/all_gather | solution.py:79
  180.3 18.0 %copy-start.2 = (f32[1,2,512,256]{3,2,1,0:T(8,128)S(1)}, f32[1,2,512,256]{3,2,1,0:T(8,128)}, u32[]{:S(2)}) copy-start(f32[1,2,512,256]{3,2,1,0:T(8,128)} %reduce-scatter.2.cloned.1.call-done) | copy-start | bytes 3145732
  186.9 1.2 collective-permute-start
  188.1 5.9 %collective-permute-start.1 = (f32[1,2,512]{2,1,0:T(2,128)S(1)}, f32[1,2,512]{2,1,0:T(2,128)S(1)}, u32[]{:S(2)}, u32[]{:S(2)}) collective-permute-start(f32[1,2,512]{2,1,0:T(2,128)S(1)} %fusion.76), channel_id=1, source_target_pairs={{0,4},{2,6},{4,0},{6,2},{1,5},{3,7},{5,1},{7,3},{8,12},{10,14},{12... | collective-permute-start | bytes 12296 | tf_op jit(solution)/shard_map/ppermute | solution.py:16
  198.9 14.0 %copy-start.8 = (s32[4]{0:T(128)S(1)}, s32[4]{0:T(128)}, u32[]{:S(2)}) copy-start(s32[4]{0:T(128)} %param.17) | copy-start | bytes 52
  200.6 1.2 collective-permute-start.2
  201.9 3.7 %collective-permute-start.3 = (f32[1,2,512]{2,1,0:T(2,128)S(1)}, f32[1,2,512]{2,1,0:T(2,128)S(1)}, u32[]{:S(2)}, u32[]{:S(2)}) collective-permute-start(f32[1,2,512]{2,1,0:T(2,128)S(1)} %fusion.75), channel_id=1, source_target_pairs={{0,4},{2,6},{4,0},{6,2},{1,5},{3,7},{5,1},{7,3},{8,12},{10,14},{12... | collective-permute-start | bytes 12296 | tf_op jit(solution)/shard_map/ppermute | solution.py:16
  212.6 1.6 collective-permute-start.4
  214.2 3.7 %collective-permute-start.5 = (f32[1,2,512]{2,1,0:T(2,128)S(1)}, f32[1,2,512]{2,1,0:T(2,128)S(1)}, u32[]{:S(2)}, u32[]{:S(2)}) collective-permute-start(f32[1,2,512]{2,1,0:T(2,128)S(1)} %fusion.74), channel_id=1, source_target_pairs={{0,4},{2,6},{4,0},{6,2},{1,5},{3,7},{5,1},{7,3},{8,12},{10,14},{12... | collective-permute-start | bytes 12296 | tf_op jit(solution)/shard_map/ppermute | solution.py:16
  224.7 29.1 %collective-permute-start.6 = (f32[1,2,512]{2,1,0:T(2,128)S(1)}, f32[1,2,512]{2,1,0:T(2,128)S(1)}, u32[]{:S(2)}, u32[]{:S(2)}) collective-permute-start(f32[1,2,512]{2,1,0:T(2,128)S(1)} %pad_maximum_fusion.3), channel_id=1, source_target_pairs={{0,2},{2,0},{4,6},{6,4},{1,3},{3,1},{5,7},{7,5},{8,10},{10,8},{12,... | collective-permute-start | bytes 12296 | tf_op jit(solution)/shard_map/ppermute | solution.py:16
  225.9 49.2 %copy-start.6 = (s32[4]{0:T(128)S(1)}, s32[4]{0:T(128)}, u32[]{:S(2)}) copy-start(s32[4]{0:T(128)} %param.16) | copy-start | bytes 52
  253.9 3.7 %collective-permute-start.7 = (f32[1,2,512]{2,1,0:T(2,128)S(1)}, f32[1,2,512]{2,1,0:T(2,128)S(1)}, u32[]{:S(2)}, u32[]{:S(2)}) collective-permute-start(f32[1,2,512]{2,1,0:T(2,128)S(1)} %fusion.73), channel_id=1, source_target_pairs={{0,4},{2,6},{4,0},{6,2},{1,5},{3,7},{5,1},{7,3},{8,12},{10,14},{12... | collective-permute-start | bytes 12296 | tf_op jit(solution)/shard_map/ppermute | solution.py:16
Sparse Core Ops, SparseCore 0:
  67.3 55.9 all-gather.2
  135.9 44.4 reduce-scatter.1
  194.1 55.0 all-gather.4
